TPU v7x, 256 devices: a whole 4x4x8 slice. The times are simulated.
256 devices in a mesh: row: 16 (over z, core), col: 16 (over x, y).
Axes of the slice: x: 4, y: 4, z: 8, core: 2. Of those that a mesh axis runs over, the one named last changes fastest.
Arguments:
- tiles: float32 [16, 16, 16, 128, 128], P('row', 'col'), may hold values from -1 to 1
- tile_rows: int32 [16, 16, 16], P('row', 'col'), may hold values from 0 to 63, as said below
- tile_cols: int32 [16, 16, 16], P('row', 'col'), may hold values from 0 to 63
- tile_counts: int32 [16, 16], P('row', 'col'), may hold values from 2 to 16, as said below
- objective: float32 [131072], P('col'), may hold values from -6 to 6
- upper: float32 [131072], P('col'), may hold values from 0.2 to 2
- bound_codes: int32 [131072], P('col'), may hold values from 0 to 2
- rhs: float32 [131072], P('row'), may hold values from -6 to 6
- row_codes: int32 [131072], P('row'), may hold values from 0 to 1
Outputs:
- primal: float32 [131072], P('col')
- dual: float32 [131072], P('row')
Inputs may be any that keep to these rules, and one draw needn't show every extreme that they name: `tile_rows`: one device's live slots hold distinct (tile row, tile column) pairs. `tile_counts`: slots at or past a device's count are not part of K; some device has all 16 slots live.
All inputs are finite; a program needn't handle non-finite values. Where the computation divides by a largest or mean magnitude, that divisor is 1e-20 or more.
Results may differ from a plain program's by a relative error of at most 0.00018.
Values sent between devices are 32-bit elements; how exact they have to be, the bound alone decides.
A program may use at most 64 MiB of HBM per device.

v0:
```python
import jax
import jax.numpy as jnp
from jax import lax
from jax.sharding import PartitionSpec as P

TILE_BLOCK = 16
TILE_ROWS = 64
TILE_COLS = 64
OUTER = 2
INNER = 4


def project_primal(values, bound_codes, upper):
    values = jnp.where(bound_codes >= 1, jnp.maximum(values, 0.0), values)
    return jnp.where(bound_codes == 2, jnp.minimum(values, upper), values)


def project_dual(values, row_codes):
    return jnp.where(row_codes == 1, jnp.maximum(values, 0.0), values)


def step_update(step_size, weight, inter_term, primal_sq, dual_sq, counter):
    shrink = 1.0 - (counter + 1) ** (-0.3)
    growth = 1.0 + (counter + 1) ** (-0.6)
    numer = shrink * (weight * primal_sq + dual_sq / weight + 1e-06)
    return numer / jnp.maximum(2.0 * jnp.abs(inter_term), numer / (growth * step_size))


def tile_products(tile_data, row_slots, col_slots, live_count, vector, direction):
    highest = lax.Precision.HIGHEST
    width = tile_data.shape[-1]
    groups = (live_count + TILE_BLOCK - 1) // TILE_BLOCK
    if direction == "forward":
        shaped = vector.reshape(TILE_COLS, width)
        out_rows = TILE_ROWS
    else:
        shaped = vector.reshape(TILE_ROWS, width)
        out_rows = TILE_COLS

    def visit(group, total):
        first_slot = group * TILE_BLOCK
        alive = (first_slot + jnp.arange(TILE_BLOCK, dtype=jnp.int32) < live_count).astype(
            jnp.float32
        )
        row_hot = (row_slots[:, None] == jnp.arange(TILE_ROWS, dtype=jnp.int32)[None, :]).astype(
            jnp.float32
        )
        col_hot = (col_slots[:, None] == jnp.arange(TILE_COLS, dtype=jnp.int32)[None, :]).astype(
            jnp.float32
        )
        if direction == "forward":
            pieces = jnp.dot(col_hot, shaped, precision=highest)
            images = jnp.einsum("tij,tj->ti", tile_data, pieces, precision=highest)
            return total + jnp.einsum(
                "tk,ti->ki", row_hot * alive[:, None], images, precision=highest
            )
        else:
            pieces = jnp.dot(row_hot, shaped, precision=highest)
            images = jnp.einsum("tij,ti->tj", tile_data, pieces, precision=highest)
            return total + jnp.einsum(
                "tk,tj->kj", col_hot * alive[:, None], images, precision=highest
            )

    total = lax.fori_loop(0, groups, visit, jnp.zeros((out_rows, width), jnp.float32))
    return total.reshape(-1)


def per_device(
    tiles, tile_rows, tile_cols, tile_counts, objective, upper, bound_codes, rhs, row_codes
):
    tile_data = tiles[0, 0]
    row_slots = tile_rows[0, 0]
    col_slots = tile_cols[0, 0]
    live_count = tile_counts[0, 0]
    row_place = lax.axis_index("row")
    col_place = lax.axis_index("col")
    primal_mask = (row_place == 0).astype(jnp.float32)
    dual_mask = (col_place == 0).astype(jnp.float32)

    def forward(vector):
        partial_rows = tile_products(tile_data, row_slots, col_slots, live_count, vector, "forward")
        return lax.psum(partial_rows, "col")

    def backward(vector):
        partial_cols = tile_products(
            tile_data, row_slots, col_slots, live_count, vector, "backward"
        )
        return lax.psum(partial_cols, "row")

    def pair_sums(primal_term, dual_term):
        return lax.psum((primal_term * primal_mask, dual_term * dual_mask), ("row", "col"))

    alive_slots = (jnp.arange(tile_data.shape[0], dtype=jnp.int32) < live_count).astype(jnp.float32)
    local_largest = jnp.max(jnp.abs(tile_data) * alive_slots[:, None, None])
    largest = lax.pmax(local_largest, ("row", "col"))
    step_size = 0.05 / (largest + 1e-06)
    object_sq, rhs_sq = pair_sums(jnp.sum(objective * objective), jnp.sum(rhs * rhs))
    weight = jnp.sqrt((object_sq + 1e-06) / (rhs_sq + 1e-06))
    primal = jnp.zeros_like(objective)
    dual_piece = jnp.zeros_like(rhs)
    row_image = jnp.zeros_like(rhs)
    col_image = jnp.zeros_like(objective)
    counter = 0
    for cycle_index in range(OUTER):
        start_primal = primal
        start_dual = dual_piece
        primal_total = jnp.zeros_like(objective)
        dual_total = jnp.zeros_like(rhs)
        weight_total = jnp.zeros((), jnp.float32)
        for step_index in range(INNER):
            counter += 1
            next_primal = project_primal(
                primal - step_size / weight * (objective - col_image), bound_codes, upper
            )
            next_row = forward(next_primal)
            next_dual = project_dual(
                dual_piece + step_size * weight * (rhs - (2.0 * next_row - row_image)), row_codes
            )
            next_col = backward(next_dual)
            primal_move = next_primal - primal
            dual_move = next_dual - dual_piece
            inter_term, primal_sq, dual_sq = lax.psum(
                (
                    jnp.sum(primal_move * (next_col - col_image)) * primal_mask,
                    jnp.sum(primal_move * primal_move) * primal_mask,
                    jnp.sum(dual_move * dual_move) * dual_mask,
                ),
                ("row", "col"),
            )
            primal_total = primal_total + step_size * next_primal
            dual_total = dual_total + step_size * next_dual
            weight_total = weight_total + step_size
            step_size = step_update(step_size, weight, inter_term, primal_sq, dual_sq, counter)
            primal, dual_piece, row_image, col_image = (next_primal, next_dual, next_row, next_col)
        primal = primal_total / weight_total
        dual_piece = dual_total / weight_total
        primal_shift = primal - start_primal
        dual_shift = dual_piece - start_dual
        primal_drift, dual_drift = pair_sums(
            jnp.sum(primal_shift * primal_shift), jnp.sum(dual_shift * dual_shift)
        )
        weight = jnp.sqrt(weight * jnp.sqrt(dual_drift + 1e-06) / jnp.sqrt(primal_drift + 1e-06))
        if cycle_index + 1 < OUTER:
            row_image = forward(primal)
            col_image = backward(dual_piece)
    return (primal, dual_piece)


def solution(mesh):
    placed = (
        P("row", "col", None, None, None),
        P("row", "col", None),
        P("row", "col", None),
        P("row", "col"),
        P("col"),
        P("col"),
        P("col"),
        P("row"),
        P("row"),
    )
    return jax.shard_map(
        per_device, mesh=mesh, in_specs=placed, out_specs=(P("col"), P("row")), check_vma=False
    )
```

profile of v0, /device:TPU:32, one launch (start us, length us, event | category | flops | bytes accessed | tf_op | source)
XLA Modules:
  0.0 1723.5 jit_solution(5136370811758483441)
XLA Ops:
  10.5 79.8 %all-reduce.7 = (f32[]{:T(128)}, f32[]{:T(128)}) all-reduce(f32[]{:T(128)S(6)} %mul.700, f32[]{:T(128)S(6)} %mul.702), channel_id=1, replica_groups=mesh['row'=16,'col'=16] {'row','col'}, use_global_device_ids=true, to_apply=%region_1.0 | all-reduce | flops 2 | bytes 16 | tf_op jit(solution)/shard_map/psum | solution.py:91
  91.7 2.2 fusion.120
  93.9 73.6 %pmax.7 = f32[]{:T(128)} all-reduce(f32[]{:T(128)} %fusion.120), channel_id=1, replica_groups=mesh['row'=16,'col'=16] {'row','col'}, use_global_device_ids=true, to_apply=%region_5.0 | all-reduce | flops 1 | bytes 8 | tf_op jit(solution)/shard_map/pmax | solution.py:95
  169.1 1.7 fusion.117
  171.5 1.0 while.204
  172.5 70.9 %psum.297 = f32[8192]{0:T(1024)S(1)} all-reduce(f32[8192]{0:T(1024)S(1)} %bitcast.318), channel_id=1, replica_groups=mesh['row'=16,'col'=16] {'col'}, use_global_device_ids=true, to_apply=%region_10.11 | all-reduce | flops 8192 | bytes 65536 | tf_op jit(solution)/shard_map/psum | solution.py:82
  244.2 1.0 fusion.115
  245.2 1.0 while.205
  246.2 42.2 %psum.299 = f32[8192]{0:T(1024)S(1)} all-reduce(f32[8192]{0:T(1024)S(1)} %bitcast.319), channel_id=1, replica_groups=mesh['row'=16,'col'=16] {'row'}, use_global_device_ids=true, to_apply=%region_15.16 | all-reduce | flops 8192 | bytes 65536 | tf_op jit(solution)/shard_map/psum | solution.py:88
  291.1 74.6 %all-reduce.6 = (f32[]{:T(128)}, f32[]{:T(128)}, f32[]{:T(128)}) all-reduce(f32[]{:T(128)S(6)} %mul.708, f32[]{:T(128)S(6)} %mul.715, f32[]{:T(128)S(6)} %mul.717), channel_id=1, replica_groups=mesh['row'=16,'col'=16] {'row','col'}, use_global_device_ids=true, to_apply=%region_7.8 | all-reduce | flops 3 | bytes 24 | tf_op jit(solution)/shard_map/psum | solution.py:122
  367.9 1.7 fusion.113
  369.6 1.0 while.206
  370.6 71.0 %psum.302 = f32[8192]{0:T(1024)S(1)} all-reduce(f32[8192]{0:T(1024)S(1)} %bitcast.320), channel_id=1, replica_groups=mesh['row'=16,'col'=16] {'col'}, use_global_device_ids=true, to_apply=%region_22.23 | all-reduce | flops 8192 | bytes 65536 | tf_op jit(solution)/shard_map/psum | solution.py:82
  442.4 1.0 fusion.111
  443.4 1.0 while.207
  444.4 42.2 %psum.304 = f32[8192]{0:T(1024)S(1)} all-reduce(f32[8192]{0:T(1024)S(1)} %bitcast.321), channel_id=1, replica_groups=mesh['row'=16,'col'=16] {'row'}, use_global_device_ids=true, to_apply=%region_27.28 | all-reduce | flops 8192 | bytes 65536 | tf_op jit(solution)/shard_map/psum | solution.py:88
  486.6 0.7 multiply_reduce_fusion.17
  489.3 74.6 %all-reduce.5 = (f32[]{:T(128)}, f32[]{:T(128)}, f32[]{:T(128)}) all-reduce(f32[]{:T(128)S(6)} %mul.722, f32[]{:T(128)S(6)} %mul.729, f32[]{:T(128)S(6)} %mul.731), channel_id=1, replica_groups=mesh['row'=16,'col'=16] {'row','col'}, use_global_device_ids=true, to_apply=%region_19.20 | all-reduce | flops 3 | bytes 24 | tf_op jit(solution)/shard_map/psum | solution.py:122
  566.1 1.7 fusion.109
  567.8 1.0 while.208
  568.8 71.0 %psum.307 = f32[8192]{0:T(1024)S(1)} all-reduce(f32[8192]{0:T(1024)S(1)} %bitcast.322), channel_id=1, replica_groups=mesh['row'=16,'col'=16] {'col'}, use_global_device_ids=true, to_apply=%region_34.35 | all-reduce | flops 8192 | bytes 65536 | tf_op jit(solution)/shard_map/psum | solution.py:82
  640.6 1.0 fusion.107
  641.6 1.0 while.209
  642.6 42.2 %psum.309 = f32[8192]{0:T(1024)S(1)} all-reduce(f32[8192]{0:T(1024)S(1)} %bitcast.323), channel_id=1, replica_groups=mesh['row'=16,'col'=16] {'row'}, use_global_device_ids=true, to_apply=%region_39.40 | all-reduce | flops 8192 | bytes 65536 | tf_op jit(solution)/shard_map/psum | solution.py:88
  684.8 0.7 multiply_reduce_fusion.14
  687.5 74.6 %all-reduce.4 = (f32[]{:T(128)}, f32[]{:T(128)}, f32[]{:T(128)}) all-reduce(f32[]{:T(128)S(6)} %mul.736, f32[]{:T(128)S(6)} %mul.743, f32[]{:T(128)S(6)} %mul.745), channel_id=1, replica_groups=mesh['row'=16,'col'=16] {'row','col'}, use_global_device_ids=true, to_apply=%region_31.32 | all-reduce | flops 3 | bytes 24 | tf_op jit(solution)/shard_map/psum | solution.py:122
  765.0 1.7 fusion.105
  766.7 1.0 while.210
  767.7 71.0 %psum.312 = f32[8192]{0:T(1024)S(1)} all-reduce(f32[8192]{0:T(1024)S(1)} %bitcast.324), channel_id=1, replica_groups=mesh['row'=16,'col'=16] {'col'}, use_global_device_ids=true, to_apply=%region_46.47 | all-reduce | flops 8192 | bytes 65536 | tf_op jit(solution)/shard_map/psum | solution.py:82
  838.7 0.7 multiply_reduce_fusion.10
  839.6 1.0 fusion.103
  840.6 1.0 while.211
  842.2 1.0 fusion.101
  843.2 1.0 while.212
  845.0 1.7 fusion.97
  846.8 1.0 while.214
  850.3 88.5 %all-reduce.15.cloned.1.call-done = (f32[8192]{0:T(1024)}, f32[8192]{0:T(1024)}) async-done(((f32[8192]{0:T(1024)}, f32[8192]{0:T(1024)}), (f32[8192]{0:T(1024)}, f32[8192]{0:T(1024)})) %all-reduce.15.cloned.1.call-update) | async-done | bytes 65552 | tf_op jit(solution)/shard_map/psum | solution.py:88
  938.8 1.4 multiply_reduce_fusion.11
  941.5 77.5 %all-reduce.3 = (f32[]{:T(128)}, f32[]{:T(128)}, f32[]{:T(128)}, f32[]{:T(128)}, f32[]{:T(128)}) all-reduce(f32[]{:T(128)S(6)} %mul.750, f32[]{:T(128)S(6)} %mul.757, f32[]{:T(128)S(6)} %mul.759, f32[]{:T(128)S(6)} %mul.775, f32[]{:T(128)S(6)} %mul.778), channel_id=1, replica_groups=mesh['row'=16,'col'=16] {'row','col'}, use_global_device_ids=true, to_apply=%region_43.44 | all-reduce | flops 5 | bytes 40 | tf_op jit(solution)/shard_map/psum | solution.py:122
  1022.6 1.7 fusion.99
  1024.3 1.0 while.213
  1026.0 88.5 %all-reduce.13.cloned.1.call-done = (f32[8192]{0:T(1024)}, f32[8192]{0:T(1024)}) async-done(((f32[8192]{0:T(1024)}, f32[8192]{0:T(1024)}), (f32[8192]{0:T(1024)}, f32[8192]{0:T(1024)})) %all-reduce.13.cloned.1.call-update) | async-done | bytes 65552 | tf_op jit(solution)/shard_map/psum | solution.py:82
  1114.5 1.4 multiply_reduce_fusion.7
  1116.1 1.0 fusion.95
  1117.1 1.0 while.215
  1118.1 43.5 %psum.323 = f32[8192]{0:T(1024)S(1)} all-reduce(f32[8192]{0:T(1024)S(1)} %bitcast.329), channel_id=1, replica_groups=mesh['row'=16,'col'=16] {'row'}, use_global_device_ids=true, to_apply=%region_73.74 | all-reduce | flops 8192 | bytes 65536 | tf_op jit(solution)/shard_map/psum | solution.py:88
  1164.2 77.8 %all-reduce.2 = (f32[]{:T(128)}, f32[]{:T(128)}, f32[]{:T(128)}) all-reduce(f32[]{:T(128)S(6)} %mul.783, f32[]{:T(128)S(6)} %mul.790, f32[]{:T(128)S(6)} %mul.792), channel_id=1, replica_groups=mesh['row'=16,'col'=16] {'row','col'}, use_global_device_ids=true, to_apply=%region_62.63 | all-reduce | flops 3 | bytes 24 | tf_op jit(solution)/shard_map/psum | solution.py:122
  1244.4 1.7 fusion.93
  1246.1 1.0 while.216
  1247.1 70.4 %psum.326 = f32[8192]{0:T(1024)S(1)} all-reduce(f32[8192]{0:T(1024)S(1)} %bitcast.330), channel_id=1, replica_groups=mesh['row'=16,'col'=16] {'col'}, use_global_device_ids=true, to_apply=%region_80.81 | all-reduce | flops 8192 | bytes 65536 | tf_op jit(solution)/shard_map/psum | solution.py:82
  1318.3 1.0 fusion.91
  1319.3 1.0 while.217
  1320.3 42.5 %psum.328 = f32[8192]{0:T(1024)S(1)} all-reduce(f32[8192]{0:T(1024)S(1)} %bitcast.331), channel_id=1, replica_groups=mesh['row'=16,'col'=16] {'row'}, use_global_device_ids=true, to_apply=%region_85.86 | all-reduce | flops 8192 | bytes 65536 | tf_op jit(solution)/shard_map/psum | solution.py:88
  1365.5 74.6 %all-reduce.1 = (f32[]{:T(128)}, f32[]{:T(128)}, f32[]{:T(128)}) all-reduce(f32[]{:T(128)S(6)} %mul.799, f32[]{:T(128)S(6)} %mul.806, f32[]{:T(128)S(6)} %mul.808), channel_id=1, replica_groups=mesh['row'=16,'col'=16] {'row','col'}, use_global_device_ids=true, to_apply=%region_77.78 | all-reduce | flops 3 | bytes 24 | tf_op jit(solution)/shard_map/psum | solution.py:122
  1442.4 1.7 fusion.89
  1444.2 1.0 while.218
  1445.2 71.0 %psum.331 = f32[8192]{0:T(1024)S(1)} all-reduce(f32[8192]{0:T(1024)S(1)} %bitcast.332), channel_id=1, replica_groups=mesh['row'=16,'col'=16] {'col'}, use_global_device_ids=true, to_apply=%region_92.93 | all-reduce | flops 8192 | bytes 65536 | tf_op jit(solution)/shard_map/psum | solution.py:82
  1516.9 1.0 fusion.87
  1517.9 1.0 while.219
  1518.9 43.1 %psum.333 = f32[8192]{0:T(1024)S(1)} all-reduce(f32[8192]{0:T(1024)S(1)} %bitcast.333), channel_id=1, replica_groups=mesh['row'=16,'col'=16] {'row'}, use_global_device_ids=true, to_apply=%region_97.98 | all-reduce | flops 8192 | bytes 65536 | tf_op jit(solution)/shard_map/psum | solution.py:88
  1564.7 74.6 %all-reduce = (f32[]{:T(128)}, f32[]{:T(128)}, f32[]{:T(128)}) all-reduce(f32[]{:T(128)S(6)} %mul.815, f32[]{:T(128)S(6)} %mul.822, f32[]{:T(128)S(6)} %mul.824), channel_id=1, replica_groups=mesh['row'=16,'col'=16] {'row','col'}, use_global_device_ids=true, to_apply=%region_89.90 | all-reduce | flops 3 | bytes 24 | tf_op jit(solution)/shard_map/psum | solution.py:122
  1642.3 1.7 fusion.85
  1644.0 1.0 while.220
  1645.0 71.0 %psum.335 = f32[8192]{0:T(1024)S(1)} all-reduce(f32[8192]{0:T(1024)S(1)} %bitcast.317), channel_id=1, replica_groups=mesh['row'=16,'col'=16] {'col'}, use_global_device_ids=true, to_apply=%region_102.103 | all-reduce | flops 8192 | bytes 65536 | tf_op jit(solution)/shard_map/psum | solution.py:82
  (122 shorter events, 32.4 us)
Async XLA Ops:
  7.2 0.8 copy-start.1
  7.2 1.4 copy-start.2
  7.2 161.9 %copy-start = (f32[1,1,16,128,128]{4,3,2,1,0:T(8,128)S(1)}, f32[1,1,16,128,128]{4,3,2,1,0:T(8,128)}, u32[]{:S(2)}) copy-start(f32[1,1,16,128,128]{4,3,2,1,0:T(8,128)} %param.43) | copy-start | bytes 3145732
  7.2 931.6 %all-reduce.15.cloned.1.call-start = ((), (), s32[]{:S(2)}) async-start(), calls=%async_computation.1 | async-start | bytes 131072 | tf_op jit(solution)/shard_map/psum | solution.py:88
  91.7 76.6 %copy-start.3 = (f32[8192]{0:T(1024)S(1)}, f32[8192]{0:T(1024)}, u32[]{:S(2)}) copy-start(f32[8192]{0:T(1024)} %param.48) | copy-start | bytes 98308
  91.7 76.6 %copy-start.11 = (s32[8192]{0:T(1024)S(1)}, s32[8192]{0:T(1024)}, u32[]{:S(2)}) copy-start(s32[8192]{0:T(1024)} %param.49) | copy-start | bytes 98308
  168.3 0.7 copy-start.12
  170.9 0.7 copy-start.13
  172.5 70.9 %copy-start.10 = (s32[8192]{0:T(1024)S(1)}, s32[8192]{0:T(1024)}, u32[]{:S(2)}) copy-start(s32[8192]{0:T(1024)} %param.51) | copy-start | bytes 98308
  841.6 0.6 copy-start.4
  844.1 0.6 copy-start.5
  844.8 269.7 %all-reduce.13.cloned.1.call-start = ((), (), s32[]{:S(2)}) async-start(), calls=%async_computation | async-start | bytes 131072 | tf_op jit(solution)/shard_map/psum | solution.py:82
  847.8 0.6 copy-start.6
  940.2 82.1 %copy-start.8 = (f32[8192]{0:T(1024)S(1)}, f32[8192]{0:T(1024)}, u32[]{:S(2)}) copy-start(f32[8192]{0:T(1024)} %get-tuple-element.1828) | copy-start | bytes 98308
  1025.3 0.6 copy-start.7
  1247.1 70.4 %copy-start.9 = (f32[8192]{0:T(1024)S(1)}, f32[8192]{0:T(1024)}, u32[]{:S(2)}) copy-start(f32[8192]{0:T(1024)} %get-tuple-element.1827) | copy-start | bytes 98308
Sparse Core Ops, SparseCore 0:
  844.9 93.8 all-reduce.14
  1026.1 88.3 all-reduce.12
where the time goes:
time: 1730 us; the launch traced here: 1720 us
  blocking collectives  1430 us (83%)
  waiting for transfers between devices  177 us (10%)
  between operations  49.5 us (3%)
  matrix products  31.9 us (2%)
  other arithmetic  28 us (2%)
    psum x7, blocking collectives, per_device(): lax.psum((jnp.sum(primal_move * (next_col - col_image)) * primal_mask, jn...  528 us
    psum x7, blocking collectives, forward(): return lax.psum(partial_rows, 'col')  496 us
    psum x6, blocking collectives, backward(): return lax.psum(partial_cols, 'row')  256 us
    psum x1, waiting for transfers between devices, backward(): return lax.psum(partial_cols, 'row')  88.5 us
    psum x1, waiting for transfers between devices, forward(): return lax.psum(partial_rows, 'col')  88.5 us
    psum x1, blocking collectives, pair_sums(): lax.psum((primal_term * primal_mask, dual_term * dual_mask), ('row', 'col'))  79.8 us
    pmax x1, blocking collectives, per_device(): largest = lax.pmax(local_largest, ('row', 'col'))  73.6 us
  transfers between devices with their start and end apart: 2, of which 2 were waited for; matrix products, arithmetic and copies ran while one was open for 0% of the time, Pallas kernels for 0%

commit v1 on v0

--- a/solution.py
+++ b/solution.py
@@ -120,12 +120,15 @@
             primal_move = next_primal - primal
             dual_move = next_dual - dual_piece
             inter_term, primal_sq, dual_sq = lax.psum(
-                (
-                    jnp.sum(primal_move * (next_col - col_image)) * primal_mask,
-                    jnp.sum(primal_move * primal_move) * primal_mask,
-                    jnp.sum(dual_move * dual_move) * dual_mask,
+                lax.psum(
+                    (
+                        jnp.sum(primal_move * (next_col - col_image)) * primal_mask,
+                        jnp.sum(primal_move * primal_move) * primal_mask,
+                        jnp.sum(dual_move * dual_move) * dual_mask,
+                    ),
+                    "row",
                 ),
-                ("row", "col"),
+                "col",
             )
             primal_total = primal_total + step_size * next_primal
             dual_total = dual_total + step_size * next_dual

time: 1730 us -> 1690 us (0.977)
  waiting for transfers between devices: 177 us -> 87.1 us
  blocking collectives: 1430 us -> 1490 us
    psum x7 -> x6, blocking collectives: 528 us -> 145 us  [per_device(): lax.psum((jnp.sum(primal_move * (next_col - col_image)) * primal_mask, jn...]
    psum x0 -> x7, blocking collectives: none -> 256 us  [per_device(): lax.psum(lax.psum((jnp.sum(primal_move * (next_col - col_image)) * primal...]
    psum x6 -> x8, blocking collectives: 256 us -> 360 us  [backward(): return lax.psum(partial_cols, 'row')]
    psum x1 -> x0, waiting for transfers between devices: 88.5 us -> none  [backward(): return lax.psum(partial_cols, 'row')]
    psum x1 -> x2, blocking collectives: 79.8 us -> 157 us  [pair_sums(): lax.psum((primal_term * primal_mask, dual_term * dual_mask), ('row', 'col'))]
  transfers between devices with their start and end apart: 2 -> 1, of which waited for: 2 -> 1; matrix products, arithmetic and copies ran while one was open for 0% -> 0% of each run, Pallas kernels for 0% -> 0%
where the time goes in v1:
time: 1690 us
  blocking collectives  1490 us (88%)
  waiting for transfers between devices  87.1 us (5%)
  between operations  49.2 us (3%)
  matrix products  31.9 us (2%)
  other arithmetic  27.2 us (2%)
    psum x7, blocking collectives, forward(): return lax.psum(partial_rows, 'col')  498 us
    psum x8, blocking collectives, backward(): return lax.psum(partial_cols, 'row')  360 us
    psum x7, blocking collectives, per_device(): lax.psum(lax.psum((jnp.sum(primal_move * (next_col - col_image)) * primal...  256 us
    psum x2, blocking collectives, pair_sums(): lax.psum((primal_term * primal_mask, dual_term * dual_mask), ('row', 'col'))  157 us
    psum x6, blocking collectives, per_device(): lax.psum((jnp.sum(primal_move * (next_col - col_image)) * primal_mask, jn...  145 us
    psum x1, waiting for transfers between devices, forward(): return lax.psum(partial_rows, 'col')  87.1 us
    pmax x1, blocking collectives, per_device(): largest = lax.pmax(local_largest, ('row', 'col'))  73.6 us
  transfers between devices with their start and end apart: 1, of which 1 were waited for; matrix products, arithmetic and copies ran while one was open for 0% of the time, Pallas kernels for 0%

profile of v1, /device:TPU:32, one launch (start us, length us, event | category | flops | bytes accessed | tf_op | source)
XLA Modules:
  0.0 1686.9 jit_solution(3763424420883263469)
XLA Ops:
  10.5 79.8 %all-reduce.1 = (f32[]{:T(128)}, f32[]{:T(128)}) all-reduce(f32[]{:T(128)S(6)} %mul.700, f32[]{:T(128)S(6)} %mul.702), channel_id=1, replica_groups=mesh['row'=16,'col'=16] {'row','col'}, use_global_device_ids=true, to_apply=%region_1.0 | all-reduce | flops 2 | bytes 16 | tf_op jit(solution)/shard_map/psum | solution.py:91
  91.7 2.2 fusion.120
  93.9 73.6 %pmax.7 = f32[]{:T(128)} all-reduce(f32[]{:T(128)} %fusion.120), channel_id=1, replica_groups=mesh['row'=16,'col'=16] {'row','col'}, use_global_device_ids=true, to_apply=%region_5.0 | all-reduce | flops 1 | bytes 8 | tf_op jit(solution)/shard_map/pmax | solution.py:95
  169.1 1.7 fusion.117
  172.5 70.9 %psum.445 = f32[8192]{0:T(1024)S(1)} all-reduce(f32[8192]{0:T(1024)S(1)} %bitcast.318), channel_id=1, replica_groups=mesh['row'=16,'col'=16] {'col'}, use_global_device_ids=true, to_apply=%region_11.12 | all-reduce | flops 8192 | bytes 65536 | tf_op jit(solution)/shard_map/psum | solution.py:82
  244.2 1.0 fusion.115
  246.2 42.2 %psum.448 = f32[8192]{0:T(1024)S(1)} all-reduce(f32[8192]{0:T(1024)S(1)} %bitcast.319), channel_id=1, replica_groups=mesh['row'=16,'col'=16] {'row'}, use_global_device_ids=true, to_apply=%region_17.18 | all-reduce | flops 8192 | bytes 65536 | tf_op jit(solution)/shard_map/psum | solution.py:88
  291.1 24.1 %all-reduce.16 = (f32[]{:T(128)}, f32[]{:T(128)}, f32[]{:T(128)}) all-reduce(f32[]{:T(128)S(6)} %mul.708, f32[]{:T(128)S(6)} %mul.715, f32[]{:T(128)S(6)} %mul.717), channel_id=1, replica_groups=mesh['row'=16,'col'=16] {'row'}, use_global_device_ids=true, to_apply=%region_7.8 | all-reduce | flops 3 | bytes 24 | tf_op jit(solution)/shard_map/psum | solution.py:123
  315.2 36.1 %all-reduce.9 = (f32[]{:T(128)}, f32[]{:T(128)}, f32[]{:T(128)}) all-reduce(f32[]{:T(128)} %get-tuple-element.1847, f32[]{:T(128)} %get-tuple-element.1848, f32[]{:T(128)} %get-tuple-element.1849), channel_id=1, replica_groups=mesh['row'=16,'col'=16] {'col'}, use_global_device_ids=true, to_apply=%region_8.9 | all-reduce | flops 3 | bytes 24 | tf_op jit(solution)/shard_map/psum | solution.py:122
  353.6 1.7 fusion.113
  355.3 1.0 while.206
  356.3 71.4 %psum.453 = f32[8192]{0:T(1024)S(1)} all-reduce(f32[8192]{0:T(1024)S(1)} %bitcast.320), channel_id=1, replica_groups=mesh['row'=16,'col'=16] {'col'}, use_global_device_ids=true, to_apply=%region_26.27 | all-reduce | flops 8192 | bytes 65536 | tf_op jit(solution)/shard_map/psum | solution.py:82
  428.5 1.0 fusion.111
  429.5 1.0 while.207
  430.5 45.7 %psum.456 = f32[8192]{0:T(1024)S(1)} all-reduce(f32[8192]{0:T(1024)S(1)} %bitcast.321), channel_id=1, replica_groups=mesh['row'=16,'col'=16] {'row'}, use_global_device_ids=true, to_apply=%region_32.33 | all-reduce | flops 8192 | bytes 65536 | tf_op jit(solution)/shard_map/psum | solution.py:88
  478.9 24.1 %all-reduce.15 = (f32[]{:T(128)}, f32[]{:T(128)}, f32[]{:T(128)}) all-reduce(f32[]{:T(128)S(6)} %mul.722, f32[]{:T(128)S(6)} %mul.729, f32[]{:T(128)S(6)} %mul.731), channel_id=1, replica_groups=mesh['row'=16,'col'=16] {'row'}, use_global_device_ids=true, to_apply=%region_22.23 | all-reduce | flops 3 | bytes 24 | tf_op jit(solution)/shard_map/psum | solution.py:123
  503.0 36.1 %all-reduce.8 = (f32[]{:T(128)}, f32[]{:T(128)}, f32[]{:T(128)}) all-reduce(f32[]{:T(128)} %get-tuple-element.1844, f32[]{:T(128)} %get-tuple-element.1845, f32[]{:T(128)} %get-tuple-element.1846), channel_id=1, replica_groups=mesh['row'=16,'col'=16] {'col'}, use_global_device_ids=true, to_apply=%region_23.24 | all-reduce | flops 3 | bytes 24 | tf_op jit(solution)/shard_map/psum | solution.py:122
  541.4 1.7 fusion.109
  543.1 1.0 while.208
  544.1 71.4 %psum.461 = f32[8192]{0:T(1024)S(1)} all-reduce(f32[8192]{0:T(1024)S(1)} %bitcast.322), channel_id=1, replica_groups=mesh['row'=16,'col'=16] {'col'}, use_global_device_ids=true, to_apply=%region_41.42 | all-reduce | flops 8192 | bytes 65536 | tf_op jit(solution)/shard_map/psum | solution.py:82
  616.4 1.0 fusion.107
  617.3 1.0 while.209
  618.3 45.7 %psum.464 = f32[8192]{0:T(1024)S(1)} all-reduce(f32[8192]{0:T(1024)S(1)} %bitcast.323), channel_id=1, replica_groups=mesh['row'=16,'col'=16] {'row'}, use_global_device_ids=true, to_apply=%region_47.48 | all-reduce | flops 8192 | bytes 65536 | tf_op jit(solution)/shard_map/psum | solution.py:88
  666.7 24.1 %all-reduce.14 = (f32[]{:T(128)}, f32[]{:T(128)}, f32[]{:T(128)}) all-reduce(f32[]{:T(128)S(6)} %mul.736, f32[]{:T(128)S(6)} %mul.743, f32[]{:T(128)S(6)} %mul.745), channel_id=1, replica_groups=mesh['row'=16,'col'=16] {'row'}, use_global_device_ids=true, to_apply=%region_37.38 | all-reduce | flops 3 | bytes 24 | tf_op jit(solution)/shard_map/psum | solution.py:123
  690.9 36.3 %all-reduce.7 = (f32[]{:T(128)}, f32[]{:T(128)}, f32[]{:T(128)}) all-reduce(f32[]{:T(128)} %get-tuple-element.1841, f32[]{:T(128)} %get-tuple-element.1842, f32[]{:T(128)} %get-tuple-element.1843), channel_id=1, replica_groups=mesh['row'=16,'col'=16] {'col'}, use_global_device_ids=true, to_apply=%region_38.39 | all-reduce | flops 3 | bytes 24 | tf_op jit(solution)/shard_map/psum | solution.py:122
  729.9 1.7 fusion.105
  731.7 1.0 while.210
  732.7 71.4 %psum.469 = f32[8192]{0:T(1024)S(1)} all-reduce(f32[8192]{0:T(1024)S(1)} %bitcast.324), channel_id=1, replica_groups=mesh['row'=16,'col'=16] {'col'}, use_global_device_ids=true, to_apply=%region_56.57 | all-reduce | flops 8192 | bytes 65536 | tf_op jit(solution)/shard_map/psum | solution.py:82
  806.6 1.0 while.211
  807.6 45.7 %psum.472 = f32[8192]{0:T(1024)S(1)} all-reduce(f32[8192]{0:T(1024)S(1)} %bitcast.325), channel_id=1, replica_groups=mesh['row'=16,'col'=16] {'row'}, use_global_device_ids=true, to_apply=%region_62.63 | all-reduce | flops 8192 | bytes 65536 | tf_op jit(solution)/shard_map/psum | solution.py:88
  854.2 1.0 fusion.101
  855.2 1.0 while.212
  858.0 45.8 %all-reduce.13 = (f32[8192]{0:T(1024)S(1)}, f32[]{:T(128)}, f32[]{:T(128)}, f32[]{:T(128)}) all-reduce(f32[8192]{0:T(1024)S(1)} %bitcast.326, f32[]{:T(128)S(6)} %mul.750, f32[]{:T(128)S(6)} %mul.757, f32[]{:T(128)S(6)} %mul.759), channel_id=1, replica_groups=mesh['row'=16,'col'=16] {'row'}, use_global_device_ids=true, to_apply=%region_72.73 | all-reduce | flops 8195 | bytes 65560 | tf_op jit(solution)/shard_map/psum | solution.py:88
  903.8 36.2 %all-reduce.6 = (f32[]{:T(128)}, f32[]{:T(128)}, f32[]{:T(128)}) all-reduce(f32[]{:T(128)} %get-tuple-element.1838, f32[]{:T(128)} %get-tuple-element.1839, f32[]{:T(128)} %get-tuple-element.1840), channel_id=1, replica_groups=mesh['row'=16,'col'=16] {'col'}, use_global_device_ids=true, to_apply=%region_53.54 | all-reduce | flops 3 | bytes 24 | tf_op jit(solution)/shard_map/psum | solution.py:122
  943.1 77.5 %all-reduce = (f32[]{:T(128)}, f32[]{:T(128)}) all-reduce(f32[]{:T(128)S(6)} %mul.775, f32[]{:T(128)S(6)} %mul.778), channel_id=1, replica_groups=mesh['row'=16,'col'=16] {'row','col'}, use_global_device_ids=true, to_apply=%region_67.68 | all-reduce | flops 2 | bytes 16 | tf_op jit(solution)/shard_map/psum | solution.py:91
  1022.5 1.7 fusion.99
  1024.2 1.0 while.213
  1025.3 1.7 fusion.97
  1027.0 1.0 while.214
  1028.7 87.1 %all-reduce.19.cloned.1.call-done = (f32[8192]{0:T(1024)}, f32[8192]{0:T(1024)}) async-done(((f32[8192]{0:T(1024)}, f32[8192]{0:T(1024)}), (f32[8192]{0:T(1024)}, f32[8192]{0:T(1024)})) %all-reduce.19.cloned.1.call-update) | async-done | bytes 65552 | tf_op jit(solution)/shard_map/psum | solution.py:82
  1115.8 1.4 multiply_reduce_fusion.7
  1117.4 1.0 fusion.95
  1118.4 1.0 while.215
  1119.4 43.5 %psum.484 = f32[8192]{0:T(1024)S(1)} all-reduce(f32[8192]{0:T(1024)S(1)} %bitcast.329), channel_id=1, replica_groups=mesh['row'=16,'col'=16] {'row'}, use_global_device_ids=true, to_apply=%region_87.88 | all-reduce | flops 8192 | bytes 65536 | tf_op jit(solution)/shard_map/psum | solution.py:88
  1165.4 24.1 %all-reduce.12 = (f32[]{:T(128)}, f32[]{:T(128)}, f32[]{:T(128)}) all-reduce(f32[]{:T(128)S(6)} %mul.783, f32[]{:T(128)S(6)} %mul.790, f32[]{:T(128)S(6)} %mul.792), channel_id=1, replica_groups=mesh['row'=16,'col'=16] {'row'}, use_global_device_ids=true, to_apply=%region_74.75 | all-reduce | flops 3 | bytes 24 | tf_op jit(solution)/shard_map/psum | solution.py:123
  1189.5 39.0 %all-reduce.4 = (f32[]{:T(128)}, f32[]{:T(128)}, f32[]{:T(128)}) all-reduce(f32[]{:T(128)} %get-tuple-element.1834, f32[]{:T(128)} %get-tuple-element.1835, f32[]{:T(128)} %get-tuple-element.1836), channel_id=1, replica_groups=mesh['row'=16,'col'=16] {'col'}, use_global_device_ids=true, to_apply=%region_75.76 | all-reduce | flops 3 | bytes 24 | tf_op jit(solution)/shard_map/psum | solution.py:122
  1230.7 1.7 fusion.93
  1232.5 1.0 while.216
  1233.5 69.8 %psum.489 = f32[8192]{0:T(1024)S(1)} all-reduce(f32[8192]{0:T(1024)S(1)} %bitcast.330), channel_id=1, replica_groups=mesh['row'=16,'col'=16] {'col'}, use_global_device_ids=true, to_apply=%region_96.97 | all-reduce | flops 8192 | bytes 65536 | tf_op jit(solution)/shard_map/psum | solution.py:82
  1304.1 1.0 fusion.91
  1305.1 1.0 while.217
  1306.0 45.7 %psum.492 = f32[8192]{0:T(1024)S(1)} all-reduce(f32[8192]{0:T(1024)S(1)} %bitcast.331), channel_id=1, replica_groups=mesh['row'=16,'col'=16] {'row'}, use_global_device_ids=true, to_apply=%region_102.103 | all-reduce | flops 8192 | bytes 65536 | tf_op jit(solution)/shard_map/psum | solution.py:88
  1354.4 24.1 %all-reduce.11 = (f32[]{:T(128)}, f32[]{:T(128)}, f32[]{:T(128)}) all-reduce(f32[]{:T(128)S(6)} %mul.799, f32[]{:T(128)S(6)} %mul.806, f32[]{:T(128)S(6)} %mul.808), channel_id=1, replica_groups=mesh['row'=16,'col'=16] {'row'}, use_global_device_ids=true, to_apply=%region_92.93 | all-reduce | flops 3 | bytes 24 | tf_op jit(solution)/shard_map/psum | solution.py:123
  1378.6 36.1 %all-reduce.3 = (f32[]{:T(128)}, f32[]{:T(128)}, f32[]{:T(128)}) all-reduce(f32[]{:T(128)} %get-tuple-element.1831, f32[]{:T(128)} %get-tuple-element.1832, f32[]{:T(128)} %get-tuple-element.1833), channel_id=1, replica_groups=mesh['row'=16,'col'=16] {'col'}, use_global_device_ids=true, to_apply=%region_93.94 | all-reduce | flops 3 | bytes 24 | tf_op jit(solution)/shard_map/psum | solution.py:122
  1416.9 1.7 fusion.89
  1418.6 1.0 while.218
  1419.6 71.4 %psum.497 = f32[8192]{0:T(1024)S(1)} all-reduce(f32[8192]{0:T(1024)S(1)} %bitcast.332), channel_id=1, replica_groups=mesh['row'=16,'col'=16] {'col'}, use_global_device_ids=true, to_apply=%region_111.112 | all-reduce | flops 8192 | bytes 65536 | tf_op jit(solution)/shard_map/psum | solution.py:82
  1491.8 1.0 fusion.87
  1493.8 45.7 %psum.500 = f32[8192]{0:T(1024)S(1)} all-reduce(f32[8192]{0:T(1024)S(1)} %bitcast.333), channel_id=1, replica_groups=mesh['row'=16,'col'=16] {'row'}, use_global_device_ids=true, to_apply=%region_117.118 | all-reduce | flops 8192 | bytes 65536 | tf_op jit(solution)/shard_map/psum | solution.py:88
  1542.2 24.1 %all-reduce.10 = (f32[]{:T(128)}, f32[]{:T(128)}, f32[]{:T(128)}) all-reduce(f32[]{:T(128)S(6)} %mul.815, f32[]{:T(128)S(6)} %mul.822, f32[]{:T(128)S(6)} %mul.824), channel_id=1, replica_groups=mesh['row'=16,'col'=16] {'row'}, use_global_device_ids=true, to_apply=%region_107.108 | all-reduce | flops 3 | bytes 24 | tf_op jit(solution)/shard_map/psum | solution.py:123
  1566.4 36.1 %all-reduce.2 = (f32[]{:T(128)}, f32[]{:T(128)}, f32[]{:T(128)}) all-reduce(f32[]{:T(128)} %get-tuple-element.1828, f32[]{:T(128)} %get-tuple-element.1829, f32[]{:T(128)} %get-tuple-element.1830), channel_id=1, replica_groups=mesh['row'=16,'col'=16] {'col'}, use_global_device_ids=true, to_apply=%region_108.109 | all-reduce | flops 3 | bytes 24 | tf_op jit(solution)/shard_map/psum | solution.py:122
  1605.3 1.7 fusion.85
  1607.0 1.0 while.220
  1608.0 71.4 %psum.503 = f32[8192]{0:T(1024)S(1)} all-reduce(f32[8192]{0:T(1024)S(1)} %bitcast.317), channel_id=1, replica_groups=mesh['row'=16,'col'=16] {'col'}, use_global_device_ids=true, to_apply=%region_123.124 | all-reduce | flops 8192 | bytes 65536 | tf_op jit(solution)/shard_map/psum | solution.py:82
  (122 shorter events, 37.9 us)
Async XLA Ops:
  7.2 0.8 copy-start.1
  7.2 1.4 copy-start.2
  7.2 161.9 %copy-start = (f32[1,1,16,128,128]{4,3,2,1,0:T(8,128)S(1)}, f32[1,1,16,128,128]{4,3,2,1,0:T(8,128)}, u32[]{:S(2)}) copy-start(f32[1,1,16,128,128]{4,3,2,1,0:T(8,128)} %param.43) | copy-start | bytes 3145732
  7.2 1108.6 %all-reduce.19.cloned.1.call-start = ((), (), s32[]{:S(2)}) async-start(), calls=%async_computation | async-start | bytes 131072 | tf_op jit(solution)/shard_map/psum | solution.py:82
  91.7 76.6 %copy-start.3 = (f32[8192]{0:T(1024)S(1)}, f32[8192]{0:T(1024)}, u32[]{:S(2)}) copy-start(f32[8192]{0:T(1024)} %param.48) | copy-start | bytes 98308
  91.7 76.6 %copy-start.8 = (s32[8192]{0:T(1024)S(1)}, s32[8192]{0:T(1024)}, u32[]{:S(2)}) copy-start(s32[8192]{0:T(1024)} %param.49) | copy-start | bytes 98308
  168.3 0.7 copy-start.9
  170.9 0.7 copy-start.10
  172.5 70.9 %copy-start.7 = (s32[8192]{0:T(1024)S(1)}, s32[8192]{0:T(1024)}, u32[]{:S(2)}) copy-start(s32[8192]{0:T(1024)} %param.51) | copy-start | bytes 98308
  1025.2 1.7 copy-start.4
  1028.0 0.6 copy-start.5
  1233.5 69.8 %copy-start.6 = (f32[8192]{0:T(1024)S(1)}, f32[8192]{0:T(1024)}, u32[]{:S(2)}) copy-start(f32[8192]{0:T(1024)} %get-tuple-element.1815) | copy-start | bytes 98308
Sparse Core Ops, SparseCore 0:
  1028.8 87.0 all-reduce.18
